TPU v7x, 256 devices: a whole 4x4x8 slice. The times are simulated.
256 devices in a mesh: section: 2 (over core), tile: 128 (over y, x, z).
Axes of the slice: x: 4, y: 4, z: 8, core: 2. Of those that a mesh axis runs over, the one named last changes fastest.
Arguments:
- aerial_patch_grid: bfloat16 [384, 384, 768], P('tile'), may hold values from -6 to 6
- patch_conv_weight: bfloat16 [3, 4, 4, 96], replicated, may hold values from -0.875 to 0.875
- patch_bias: float32 [96], replicated, may hold values from -3 to 3
- merging_conv_weight: bfloat16 [2, 2, 96, 192], replicated, may hold values from -0.3125 to 0.3125
- merge_bias: float32 [192], replicated, may hold values from -3 to 3
- down_weight: bfloat16 [3, 3, 192, 384], replicated, may hold values from -0.15625 to 0.15625
- down_bias: float32 [384], replicated, may hold values from -3 to 3
- norm_gain: float32 [384], replicated, may hold values from 0.1 to 1.9
- spectral_filter: bfloat16 [384, 2, 384, 384], P('tile'), may hold values from -6 to 6
Outputs:
- block_output: bfloat16 [384, 384, 384], P('section', 'tile')
All inputs are finite; a program needn't handle non-finite values.
Results may differ from a plain program's by a relative error of at most 0.015.
Values may be sent and summed in bfloat16 or wider, within the bound.
A program may use at most 64 MiB of HBM per device.

v0:
```python
import math
import jax
import jax.numpy as jnp
from jax import lax
from jax.sharding import PartitionSpec as P

EPSILON = 1e-05


def from_behind(block, axis, distance):
    devices = range(lax.axis_size(axis))
    route = [(i - distance, i) for i in devices if i - distance in devices]
    return lax.ppermute(block, axis, route)


def fourier_tables(length):
    indices = jnp.arange(length, dtype=jnp.int32)
    product = indices[:, None] * indices[None, :] % length
    angles = product.astype(jnp.float32) * (2.0 * math.pi / length)
    return (jnp.cos(angles).astype(jnp.bfloat16), jnp.sin(angles).astype(jnp.bfloat16))


def one_hot_rows(indices, width):
    return (indices[:, None] == jnp.arange(width, dtype=jnp.int32)[None, :]).astype(jnp.bfloat16)


def spread_kernel(weight_rows, row_pick, row_cell, col_cell, width, out_cols):
    picked = jnp.dot(
        one_hot_rows(row_pick, weight_rows.shape[0]),
        weight_rows,
        preferred_element_type=jnp.float32,
    ).astype(jnp.bfloat16)
    col = jnp.arange(out_cols, dtype=jnp.int32)
    repeat = one_hot_rows(col % width, width).T
    full = jnp.dot(picked, repeat, preferred_element_type=jnp.float32)
    mask = row_cell[:, None] == col_cell[None, :]
    return jnp.where(mask, full, 0.0).astype(jnp.bfloat16)


def patch_kernel_matrix(patch_conv_weight):
    band_count = patch_conv_weight.shape[0]
    width = patch_conv_weight.shape[3]
    row = jnp.arange(band_count * 256, dtype=jnp.int32)
    pick = row // 256 * 16 + row // 16 % 4 * 4 + row % 4
    row_cell = row // 64 % 4 * 4 + row // 4 % 4
    col = jnp.arange(16 * width, dtype=jnp.int32)
    col_cell = col // width
    weight_rows = patch_conv_weight.reshape(band_count * 16, width)
    return spread_kernel(weight_rows, pick, row_cell, col_cell, width, 16 * width)


def merging_kernel_matrix(merging_conv_weight):
    in_width = merging_conv_weight.shape[2]
    out_width = merging_conv_weight.shape[3]
    row = jnp.arange(16 * in_width, dtype=jnp.int32)
    pos = row // in_width
    pick = (pos // 4 % 2 * 2 + pos % 2) * in_width + row % in_width
    row_cell = pos // 8 * 2 + pos // 2 % 2
    col = jnp.arange(4 * out_width, dtype=jnp.int32)
    col_cell = col // out_width
    weight_rows = merging_conv_weight.reshape(4 * in_width, out_width)
    return spread_kernel(weight_rows, pick, row_cell, col_cell, out_width, 4 * out_width)


def down_matrices(down_weight):
    nothing = jnp.zeros_like(down_weight[0, 0])
    in_width = down_weight.shape[2]
    out_width = down_weight.shape[3]

    def arrange(entries):
        return jnp.stack(
            [jnp.stack(entries[0], axis=0), jnp.stack(entries[1], axis=0)], axis=0
        ).reshape(4 * in_width, out_width)

    own_taps = arrange(
        [[down_weight[1, 1], down_weight[1, 2]], [down_weight[2, 1], down_weight[2, 2]]]
    )
    upper_taps = arrange([[nothing, nothing], [down_weight[0, 1], down_weight[0, 2]]])
    left_taps = arrange([[nothing, down_weight[1, 0]], [nothing, down_weight[2, 0]]])
    corner_taps = arrange([[nothing, nothing], [nothing, down_weight[0, 0]]])
    return (own_taps, upper_taps, left_taps, corner_taps)


def stem_layers(aerial_patch_grid, patch_conv_weight, patch_bias, merging_conv_weight, merge_bias):
    initial_layer = jnp.einsum(
        "zji,if->zjf",
        aerial_patch_grid,
        patch_kernel_matrix(patch_conv_weight),
        preferred_element_type=jnp.float32,
    )
    initial_layer = jax.nn.gelu(initial_layer + jnp.tile(patch_bias, 16), approximate=True).astype(
        jnp.bfloat16
    )
    layer_two = jnp.einsum(
        "zji,if->zjf",
        initial_layer,
        merging_kernel_matrix(merging_conv_weight),
        preferred_element_type=jnp.float32,
    )
    return jax.nn.gelu(layer_two + jnp.tile(merge_bias, 4), approximate=True).astype(jnp.bfloat16)


def rim_above(extended):
    return from_behind(extended[-1:], "tile", 1)


def down_conv(upper_rim, extended, down_weight, down_bias):
    stacked = jnp.concatenate([upper_rim, extended], axis=0)
    own_taps, upper_taps, left_taps, corner_taps = down_matrices(down_weight)
    summed = jnp.einsum(
        "rwk,kc->crw", stacked[1:, 1:], own_taps, preferred_element_type=jnp.float32
    )
    summed = summed + jnp.einsum(
        "rwk,kc->crw", stacked[:-1, 1:], upper_taps, preferred_element_type=jnp.float32
    )
    summed = summed + jnp.einsum(
        "rwk,kc->crw", stacked[1:, :-1], left_taps, preferred_element_type=jnp.float32
    )
    summed = summed + jnp.einsum(
        "rwk,kc->crw", stacked[:-1, :-1], corner_taps, preferred_element_type=jnp.float32
    )
    return (summed + down_bias[:, None, None]).astype(jnp.bfloat16)


def layer_norm(features, norm_gain):
    values = features.astype(jnp.float32)
    mean_value = jnp.mean(values, axis=0, keepdims=True)
    centered = values - mean_value
    variance = jnp.mean(centered * centered, axis=0, keepdims=True)
    return (norm_gain[:, None, None] * centered * lax.rsqrt(variance + EPSILON)).astype(
        jnp.bfloat16
    )


def filter_columns(row_spectrum, kernel, forward_h, inverse_h):
    spectrum = jnp.einsum(
        "puqh,chqw->cpuw", forward_h, row_spectrum, preferred_element_type=jnp.float32
    ).astype(jnp.bfloat16)
    spec_real = spectrum[:, 0].astype(jnp.float32)
    spec_imag = spectrum[:, 1].astype(jnp.float32)
    filter_real = kernel[:, 0].astype(jnp.float32)
    filter_imag = kernel[:, 1].astype(jnp.float32)
    weighted = jnp.stack(
        [
            filter_real * spec_real - filter_imag * spec_imag,
            filter_real * spec_imag + filter_imag * spec_real,
        ],
        axis=1,
    ).astype(jnp.bfloat16)
    return jnp.einsum(
        "qhpu,cpuw->chqw", inverse_h, weighted, preferred_element_type=jnp.float32
    ).astype(jnp.bfloat16)


def local(
    aerial_patch_grid,
    patch_conv_weight,
    patch_bias,
    merging_conv_weight,
    merge_bias,
    down_weight,
    down_bias,
    norm_gain,
    spectral_filter,
):
    section_index = lax.axis_index("section")
    field_cols = aerial_patch_grid.shape[1]
    channels = down_weight.shape[3]
    full_rows = spectral_filter.shape[2]
    half_channels = channels // 2
    cell_half = field_cols // 2
    image_part = lax.dynamic_slice_in_dim(
        aerial_patch_grid, section_index * cell_half, cell_half, 1
    )
    layer_two = stem_layers(
        image_part, patch_conv_weight, patch_bias, merging_conv_weight, merge_bias
    )
    left_column = from_behind(layer_two[:, -1:], "section", 1)
    extended = jnp.concatenate([left_column, layer_two], axis=1)
    upper_rim = rim_above(extended)
    feature_half = down_conv(upper_rim, extended, down_weight, down_bias)
    normed_half = layer_norm(feature_half, norm_gain)
    fields = lax.all_to_all(normed_half, "tile", split_axis=0, concat_axis=1, tiled=True)
    fields = lax.all_gather(fields, "section", axis=2, tiled=True)
    cos_h, sin_h = fourier_tables(full_rows)
    if full_rows == field_cols:
        cos_w, sin_w = (cos_h, sin_h)
    else:
        cos_w, sin_w = fourier_tables(field_cols)
    cos_part = lax.dynamic_slice_in_dim(cos_w, section_index * cell_half, cell_half, 1)
    sin_part = lax.dynamic_slice_in_dim(sin_w, section_index * cell_half, cell_half, 1)
    forward_table = jnp.stack([cos_part, -sin_part], axis=1)
    inverse_table = jnp.stack([cos_part, -sin_part], axis=0)
    forward_h = jnp.stack(
        [jnp.stack([cos_h, sin_h], axis=1), jnp.stack([-sin_h, cos_h], axis=1)], axis=0
    )
    inverse_h = jnp.stack(
        [jnp.stack([cos_h, -sin_h], axis=1), jnp.stack([sin_h, cos_h], axis=1)], axis=0
    )
    norm_scale = 1.0 / (full_rows * field_cols)
    kernel_part = lax.dynamic_slice_in_dim(spectral_filter, section_index * cell_half, cell_half, 3)
    frequency_rows = jnp.einsum(
        "chx,xqw->chqw", fields, forward_table, preferred_element_type=jnp.float32
    ).astype(jnp.bfloat16)
    back_rows = filter_columns(frequency_rows, kernel_part, forward_h, inverse_h)
    back_rows = lax.all_gather(back_rows, "section", axis=3, tiled=True)
    result = jnp.einsum(
        "chqw,qwv->chv", back_rows, inverse_table, preferred_element_type=jnp.float32
    )
    filtered_fields = (result * norm_scale).astype(jnp.bfloat16)
    rows_back = lax.all_to_all(filtered_fields, "tile", split_axis=1, concat_axis=0, tiled=True)
    summed = (feature_half.astype(jnp.float32) + rows_back.astype(jnp.float32)).astype(jnp.bfloat16)
    kept = lax.dynamic_slice_in_dim(summed, section_index * half_channels, half_channels, 0)
    sent = lax.dynamic_slice_in_dim(summed, (1 - section_index) * half_channels, half_channels, 0)
    received = lax.ppermute(sent, "section", [(0, 1), (1, 0)])
    return jnp.where(
        section_index == 0,
        jnp.concatenate([kept, received], axis=2),
        jnp.concatenate([received, kept], axis=2),
    )


def solution(mesh):
    return jax.shard_map(
        local,
        mesh=mesh,
        in_specs=(
            P("tile", None, None),
            P(),
            P(),
            P(),
            P(),
            P(),
            P(),
            P(),
            P("tile", None, None, None),
        ),
        out_specs=P("section", "tile", None),
        check_vma=False,
    )
```

profile of v0, /device:TPU:1, one launch (start us, length us, event | category | flops | bytes accessed | tf_op | source)
XLA Modules:
  0.0 175.3 jit_solution(6050538914939704282)
XLA Ops:
  8.3 2.5 %convolution_convert_fusion = bf16[1536,192]{0,1:T(8,128)(2,1)} fusion(bf16[384,192]{1,0:T(8,128)(2,1)} %bitcast.142, s32[1536]{0:T(1024)S(1)} %fusion.101), kind=kOutput, calls=%fused_computation.14 | convolution fusion | flops 227377152 | bytes 743424 | tf_op jit(solution)/shard_map/dot_general | solution.py:28
  10.8 3.5 %fusion.8 = bf16[768,1536,1]{1,0,2:T(8,128)(2,1)} fusion(s32[1536]{0:T(1024)S(1)} %get-tuple-element.41, s32[768]{0:T(1024)S(1)} %get-tuple-element.42, bf16[48,96]{1,0:T(8,128)(2,1)} %bitcast.143, s32[1536]{0:T(1024)S(1)} %get-tuple-element.40, s32[768]{0:T(1024)S(1)} %get-tuple-element.43), kind=kOutput, calls=%fused_computation.11 | convolution fusion | flops 237367296 | bytes 2386944 | tf_op jit(solution)/shard_map/dot_general | solution.py:35
  14.3 5.0 %fusion.7 = bf16[3,192,1536]{2,1,0:T(8,128)(2,1)} fusion(bf16[768,1536,1]{1,0,2:T(8,128)(2,1)} %fusion.8, f32[1536]{0:T(1024)S(1)} %add.318, bf16[3,384,768]{2,1,0:T(8,128)(2,1)S(1)} %copy-done, s32[]{:T(128)S(6)} %select_n.229), kind=kOutput, calls=%fused_computation.10 | convolution fusion | flops 1367801856 | bytes 5021700 | tf_op jit(solution)/shard_map/zji,if->zjf/dot_general | solution.py:85
  19.3 4.3 %fusion.17 = bf16[3,192,768]{2,1,0:T(8,128)(2,1)S(1)} fusion(bf16[3,192,1536]{2,1,0:T(8,128)(2,1)} %fusion.7, bf16[1536,192]{0,1:T(8,128)(2,1)} %convolution_convert_fusion, s32[768]{0:T(1024)S(1)} %get-tuple-element.45, s32[1536]{0:T(1024)S(1)} %fusion.94, f32[768]{0:T(1024)S(1)} %add.331, s32[768]{0:T(1024)S(1)} %get-tuple-element.44), kind=kOutput, calls=%fused_computation.23 | convolution fusion | flops 1820049408 | bytes 3259392 | tf_op jit(solution)/shard_map/zji,if->zjf/dot_general | solution.py:94
  28.9 4.0 %collective-permute-start.1 = (bf16[1,193,768]{2,1,0:T(8,128)(2,1)S(1)}, bf16[1,193,768]{2,1,0:T(8,128)(2,1)S(1)}, u32[]{:S(2)}, u32[]{:S(2)}) collective-permute-start(bf16[1,193,768]{2,1,0:T(8,128)(2,1)S(1)} %pad_maximum_fusion.8), channel_id=1, source_target_pairs={{0,1},{1,2},{2,3},{3,4},{4,5},{5,6},{6,7},{7,8},{8,9},{9,10},{10,1... | collective-permute-start | bytes 889352 | tf_op jit(solution)/shard_map/ppermute | solution.py:13
  34.7 1.7 fusion.135
  36.4 1.9 %collective-permute-done.1 = bf16[1,193,768]{2,1,0:T(8,128)(2,1)S(1)} collective-permute-done((bf16[1,193,768]{2,1,0:T(8,128)(2,1)S(1)}, bf16[1,193,768]{2,1,0:T(8,128)(2,1)S(1)}, u32[]{:S(2)}, u32[]{:S(2)}) %collective-permute-start.1) | collective-permute-done | bytes 296480 | tf_op jit(solution)/shard_map/ppermute | solution.py:13
  43.1 17.3 %all-to-all-start = ((bf16[384,3,192]{2,1,0:T(4,128)(2,1)}), bf16[384,3,192]{2,1,0:T(4,128)(2,1)S(1)}, u32[]{:S(2)}, u32[]{:S(2)}) async-start(bf16[384,3,192]{2,1,0:T(4,128)(2,1)} %copy.31), calls=%async_computation | async-start | bytes 1572864 | tf_op jit(solution)/shard_map/all_to_all | solution.py:183
  60.4 2.8 %constant_dynamic-slice_fusion = (bf16[3,1,384,192]{3,2,1,0:T(8,128)(2,1)}, bf16[3,1,384,192]{3,2,1,0:T(8,128)(2,1)}) fusion(bf16[3,2,384,384]{3,2,1,0:T(8,128)(2,1)} %param.17, s32[]{:T(128)S(6)} %select_n.229, s32[]{:T(128)S(6)} %add.349), kind=kLoop, calls=%fused_computation.233 | loop fusion | bytes 1769480 | tf_op jit(solution)/shard_map/slice | solution.py:141
  63.2 2.1 %copy.50 = bf16[3,1,384,192]{2,3,1,0:T(8,128)(2,1)} copy(bf16[3,1,384,192]{3,2,1,0:T(8,128)(2,1)} %get-tuple-element.7) | data formatting | bytes 884736
  65.3 2.1 %copy.51 = bf16[3,1,384,192]{2,3,1,0:T(8,128)(2,1)} copy(bf16[3,1,384,192]{3,2,1,0:T(8,128)(2,1)} %get-tuple-element.8) | data formatting | bytes 884736
  71.0 2.3 %fusion.77 = bf16[384,1,384]{2,0,1:T(8,128)(2,1)S(1)} fusion(), kind=kLoop, calls=%fused_computation.132 | loop fusion | flops 1916928 | bytes 294912 | tf_op jit(solution)/shard_map/neg | solution.py:195
  73.3 2.6 %sine_convert_fusion = (bf16[384,1,384]{2,0,1:T(8,128)(2,1)S(1)}, bf16[384,1,384]{2,0,1:T(8,128)(2,1)S(1)}) fusion(), kind=kLoop, calls=%fused_computation.93 | loop fusion | flops 1622016 | bytes 589824 | tf_op jit(solution)/shard_map/convert_element_type | solution.py:20
  77.4 6.4 %all-to-all-done = bf16[384,3,192]{2,1,0:T(4,128)(2,1)S(1)} async-done(((bf16[384,3,192]{2,1,0:T(4,128)(2,1)}), bf16[384,3,192]{2,1,0:T(4,128)(2,1)S(1)}, u32[]{:S(2)}, u32[]{:S(2)}) %all-to-all-start) | async-done | bytes 442400 | tf_op jit(solution)/shard_map/all_to_all | solution.py:183
  86.8 6.0 %all_gather.6 = bf16[3,384,384]{1,2,0:T(8,128)(2,1)} all-gather(bf16[3,384,192]{1,2,0:T(8,128)(2,1)S(1)} %copy.34), channel_id=1, replica_groups=mesh['section'=2,'tile'=128] {'section'}, dimensions={2}, use_global_device_ids=true | all-gather | bytes 1327104 | tf_op jit(solution)/shard_map/all_gather | solution.py:184
  92.8 4.1 %fusion.21 = bf16[3,2,384,192]{2,3,1,0:T(8,128)(2,1)} fusion(bf16[1,384,2,384]{3,1,2,0:T(8,128)(2,1)} %get-tuple-element.29, bf16[1,384,2,384]{3,1,2,0:T(8,128)(2,1)} %get-tuple-element.22, bf16[3,384,384]{1,2,0:T(8,128)(2,1)} %all_gather.6, bf16[384,1,192]{0,2,1:T(8,128)(2,1)} %get-tuple-element.21, bf16[384,1,192]{0,2,1:T(8,128)(2,1)} %get-tuple-element.19), kind=kOutput, calls=%fused_computation.35 | convolution fusion | flops 1023049728 | bytes 3244032 | tf_op jit(solution)/shard_map/puqh,chqw->cpuw/dot_general | solution.py:136
  98.5 1.8 %fusion.22 = bf16[3,384,2,192]{1,3,2,0:T(8,128)(2,1)} fusion(bf16[1,384,2,384]{3,1,2,0:T(8,128)(2,1)S(1)} %copy-done.6, bf16[1,384,2,384]{3,1,2,0:T(8,128)(2,1)S(1)} %copy-done.7, bf16[3,1,384,192]{2,3,1,0:T(8,128)(2,1)S(1)} %get-tuple-element.6, bf16[3,1,384,192]{2,3,1,0:T(8,128)(2,1)S(1)} %get-tuple-element.5), kind=kOutput, calls=%fused_computation.36 | convolution fusion | flops 684048384 | bytes 2949120 | tf_op jit(solution)/shard_map/qhpu,cpuw->chqw/dot_general | solution.py:150
  100.4 9.3 %all-gather.2.cloned.1.call-done = bf16[3,384,2,384]{1,3,2,0:T(8,128)(2,1)} async-done(((bf16[3,384,2,192]{1,3,2,0:T(8,128)(2,1)}), bf16[3,384,2,384]{1,3,2,0:T(8,128)(2,1)}) %all-gather.2.cloned.1.call-update) | async-done | bytes 1769488 | tf_op jit(solution)/shard_map/all_gather | solution.py:206
  109.6 2.0 %fusion.24 = bf16[3,384,192]{1,2,0:T(8,128)(2,1)S(1)} fusion(bf16[3,384,2,384]{1,3,2,0:T(8,128)(2,1)} %all-gather.2.cloned.1.call-done, bf16[1,384,192]{1,2,0:T(8,128)(2,1)S(1)} %get-tuple-element.20, bf16[1,384,192]{1,2,0:T(8,128)(2,1)S(1)} %get-tuple-element.18), kind=kOutput, calls=%fused_computation.39 | convolution fusion | flops 340770816 | bytes 2506752 | tf_op jit(solution)/shard_map/chqw,qwv->chv/dot_general | solution.py:207
  113.1 13.6 %all-to-all-start.1 = ((bf16[3,384,192]{2,0,1:T(4,128)(2,1)}), bf16[3,384,192]{2,0,1:T(4,128)(2,1)S(1)}, u32[]{:S(2)}, u32[]{:S(2)}) async-start(bf16[3,384,192]{2,0,1:T(4,128)(2,1)} %copy.35), calls=%async_computation.1 | async-start | bytes 1572864 | tf_op jit(solution)/shard_map/all_to_all | solution.py:211
  126.7 25.4 %all-to-all-done.1 = bf16[3,384,192]{2,0,1:T(4,128)(2,1)S(1)} async-done(((bf16[3,384,192]{2,0,1:T(4,128)(2,1)}), bf16[3,384,192]{2,0,1:T(4,128)(2,1)S(1)}, u32[]{:S(2)}, u32[]{:S(2)}) %all-to-all-start.1) | async-done | bytes 442400 | tf_op jit(solution)/shard_map/all_to_all | solution.py:211
  156.2 3.4 %copy.38 = f32[128,3,3,192]{3,1,0,2:T(4,128)} copy(f32[128,3,3,192]{3,2,0,1:T(4,128)} %bitcast.136) | data formatting | bytes 1769472 | tf_op jit(solution)/shard_map/convert_element_type | solution.py:212
  159.5 1.8 reshape.333
  164.1 1.9 %collective-permute-start.2 = (bf16[192,3,192]{0,2,1:T(8,128)(2,1)S(1)}, bf16[192,3,192]{0,2,1:T(8,128)(2,1)S(1)}, u32[]{:S(2)}, u32[]{:S(2)}) collective-permute-start(bf16[192,3,192]{0,2,1:T(8,128)(2,1)S(1)} %get-tuple-element.27), channel_id=1, source_target_pairs={{0,128},{128,0},{1,129},{129,1},{2,130},{130,2},{3,131},{131,3},{4... | collective-permute-start | bytes 663560 | tf_op jit(solution)/shard_map/ppermute | solution.py:215
  (70 shorter events, 33.9 us)
Async XLA Ops:
  6.5 7.8 %copy-start = (bf16[3,384,768]{2,1,0:T(8,128)(2,1)S(1)}, bf16[3,384,768]{2,1,0:T(8,128)(2,1)}, u32[]{:S(2)}) copy-start(bf16[3,384,768]{2,1,0:T(8,128)(2,1)} %param.9) | copy-start | bytes 5308420
  23.6 5.2 %collective-permute-start = (bf16[3,1,768]{2,1,0:T(2,128)(2,1)S(1)}, bf16[3,1,768]{2,1,0:T(2,128)(2,1)S(1)}, u32[]{:S(2)}, u32[]{:S(2)}) collective-permute-start(bf16[3,1,768]{2,1,0:T(2,128)(2,1)S(1)} %slice.72), channel_id=1, source_target_pairs={{0,128},{1,129},{2,130},{3,131},{4,132},{5,133},{6,134},{7,135},{8... | collective-permute-start | bytes 13832 | tf_op jit(solution)/shard_map/ppermute | solution.py:13
  28.9 9.4 %collective-permute-start.1 = (bf16[1,193,768]{2,1,0:T(8,128)(2,1)S(1)}, bf16[1,193,768]{2,1,0:T(8,128)(2,1)S(1)}, u32[]{:S(2)}, u32[]{:S(2)}) collective-permute-start(bf16[1,193,768]{2,1,0:T(8,128)(2,1)S(1)} %pad_maximum_fusion.8), channel_id=1, source_target_pairs={{0,1},{1,2},{2,3},{3,4},{4,5},{5,6},{6,7},{7,8},{8,9},{9,10},{10,1... | collective-permute-start | bytes 889352 | tf_op jit(solution)/shard_map/ppermute | solution.py:13
  36.4 2.2 %copy-start.3 = (bf16[2,2,192,384]{3,2,1,0:T(8,128)(2,1)S(1)}, bf16[2,2,192,384]{3,2,1,0:T(8,128)(2,1)}, u32[]{:S(2)}) copy-start(bf16[2,2,192,384]{3,2,1,0:T(8,128)(2,1)} %stack.125) | copy-start | bytes 1769476
  38.5 1.1 copy-start.1
  39.2 1.1 copy-start.2
  39.2 1.1 copy-start.8
  40.3 1.2 copy-start.9
  43.1 40.7 %all-to-all-start = ((bf16[384,3,192]{2,1,0:T(4,128)(2,1)}), bf16[384,3,192]{2,1,0:T(4,128)(2,1)S(1)}, u32[]{:S(2)}, u32[]{:S(2)}) async-start(bf16[384,3,192]{2,1,0:T(4,128)(2,1)} %copy.31), calls=%async_computation | async-start | bytes 1572864 | tf_op jit(solution)/shard_map/all_to_all | solution.py:183
  60.4 49.3 %all-gather.2.cloned.1.call-start = ((), (), s32[]{:S(2)}) async-start(), calls=%async_computation.2 | async-start | bytes 2654208 | tf_op jit(solution)/shard_map/all_gather | solution.py:206
  92.8 4.1 %copy-start.4 = (bf16[3,1,384,192]{2,3,1,0:T(8,128)(2,1)S(1)}, bf16[3,1,384,192]{2,3,1,0:T(8,128)(2,1)}, u32[]{:S(2)}) copy-start(bf16[3,1,384,192]{2,3,1,0:T(8,128)(2,1)} %copy.50) | copy-start | bytes 1327108
  92.8 4.1 %copy-start.5 = (bf16[3,1,384,192]{2,3,1,0:T(8,128)(2,1)S(1)}, bf16[3,1,384,192]{2,3,1,0:T(8,128)(2,1)}, u32[]{:S(2)}) copy-start(bf16[3,1,384,192]{2,3,1,0:T(8,128)(2,1)} %copy.51) | copy-start | bytes 1327108
  96.9 1.6 copy-start.6
  96.9 1.6 copy-start.7
  113.1 39.0 %all-to-all-start.1 = ((bf16[3,384,192]{2,0,1:T(4,128)(2,1)}), bf16[3,384,192]{2,0,1:T(4,128)(2,1)S(1)}, u32[]{:S(2)}, u32[]{:S(2)}) async-start(bf16[3,384,192]{2,0,1:T(4,128)(2,1)} %copy.35), calls=%async_computation.1 | async-start | bytes 1572864 | tf_op jit(solution)/shard_map/all_to_all | solution.py:211
  164.1 3.2 %collective-permute-start.2 = (bf16[192,3,192]{0,2,1:T(8,128)(2,1)S(1)}, bf16[192,3,192]{0,2,1:T(8,128)(2,1)S(1)}, u32[]{:S(2)}, u32[]{:S(2)}) collective-permute-start(bf16[192,3,192]{0,2,1:T(8,128)(2,1)S(1)} %get-tuple-element.27), channel_id=1, source_target_pairs={{0,128},{128,0},{1,129},{129,1},{2,130},{130,2},{3,131},{131,3},{4... | collective-permute-start | bytes 663560 | tf_op jit(solution)/shard_map/ppermute | solution.py:215
Sparse Core Ops, SparseCore 0:
  100.5 9.1 all-gather.1
where the time goes:
time: 176 us; the launch traced here: 175 us
  waiting for transfers between devices  44.7 us (25%)
  starting transfers between devices  38.1 us (22%)
  local copies, waits for them, and re-layouts  29.9 us (17%)
  matrix products  27 us (15%)
  other arithmetic  15.9 us (9%)
  between operations  13.7 us (8%)
  blocking collectives  6.01 us (3%)
    all_to_all x1, waiting for transfers between devices, local(): lax.all_to_all(filtered_fields, 'tile', split_axis=1, concat_axis=0, tile...  25.4 us
    all_to_all x1, starting transfers between devices, local(): lax.all_to_all(normed_half, 'tile', split_axis=0, concat_axis=1, tiled=True)  17.3 us
    all_to_all x1, starting transfers between devices, local(): lax.all_to_all(filtered_fields, 'tile', split_axis=1, concat_axis=0, tile...  13.6 us
    all_gather x1, waiting for transfers between devices, local(): back_rows = lax.all_gather(back_rows, 'section', axis=3, tiled=True)  9.27 us
    convert_element_type x5, local copies, waits for them, and re-layouts, local(): rows_back.astype(jnp.float32)  9.11 us
    all_to_all x1, waiting for transfers between devices, local(): lax.all_to_all(normed_half, 'tile', split_axis=0, concat_axis=1, tiled=True)  6.44 us
    all_gather x1, blocking collectives, local(): fields = lax.all_gather(fields, 'section', axis=2, tiled=True)  6.01 us
    ppermute x2, starting transfers between devices, from_behind(): return lax.ppermute(block, axis, route)  5.25 us
  transfers between devices with their start and end apart: 6, of which 6 were waited for; matrix products, arithmetic and copies ran while one was open for 14% of the time, Pallas kernels for 0%

commit v1 on v0

--- a/solution.py
+++ b/solution.py
@@ -181,7 +181,9 @@
     feature_half = down_conv(upper_rim, extended, down_weight, down_bias)
     normed_half = layer_norm(feature_half, norm_gain)
     fields = lax.all_to_all(normed_half, "tile", split_axis=0, concat_axis=1, tiled=True)
-    fields = lax.all_gather(fields, "section", axis=2, tiled=True)
+    fields = jnp.concatenate(
+        lax.all_to_all(jnp.stack([fields] * lax.axis_size("section")), "section", 0, 0), axis=2
+    )
     cos_h, sin_h = fourier_tables(full_rows)
     if full_rows == field_cols:
         cos_w, sin_w = (cos_h, sin_h)

time: 176 us -> 184 us (1.045)
  blocking collectives: 6.01 us -> 9.11 us
  local copies, waits for them, and re-layouts: 29.9 us -> 32.8 us
    all_to_all x0 -> x1, blocking collectives: none -> 9.11 us  [local(): lax.all_to_all(jnp.stack([fields] * lax.axis_size('section')), 'section',...]
    all_gather x1 -> x0, blocking collectives: 6.01 us -> none  [local(): fields = lax.all_gather(fields, 'section', axis=2, tiled=True)]
    another operation x0 -> x2, local copies, waits for them, and re-layouts: none -> 3.56 us  [local(): jnp.stack([fields] * lax.axis_size('section'))]
    unnamed x22 -> x28, local copies, waits for them, and re-layouts: 4.61 us -> 4.63 us
  transfers between devices with their start and end apart: 6 -> 6, of which waited for: 6 -> 6; matrix products, arithmetic and copies ran while one was open for 14% -> 13% of each run, Pallas kernels for 0% -> 0%
where the time goes in v1:
time: 184 us; the launch traced here: 183 us
  waiting for transfers between devices  44.6 us (24%)
  starting transfers between devices  38.1 us (21%)
  local copies, waits for them, and re-layouts  32.8 us (18%)
  matrix products  26.9 us (15%)
  other arithmetic  17.5 us (10%)
  between operations  13.7 us (7%)
  blocking collectives  9.11 us (5%)
    all_to_all x1, waiting for transfers between devices, local(): lax.all_to_all(filtered_fields, 'tile', split_axis=1, concat_axis=0, tile...  25.4 us
    all_to_all x1, starting transfers between devices, local(): lax.all_to_all(normed_half, 'tile', split_axis=0, concat_axis=1, tiled=True)  17.3 us
    all_to_all x1, starting transfers between devices, local(): lax.all_to_all(filtered_fields, 'tile', split_axis=1, concat_axis=0, tile...  13.6 us
    all_gather x1, waiting for transfers between devices, local(): back_rows = lax.all_gather(back_rows, 'section', axis=3, tiled=True)  9.33 us
    convert_element_type x5, local copies, waits for them, and re-layouts, local(): rows_back.astype(jnp.float32)  9.12 us
    all_to_all x1, blocking collectives, local(): lax.all_to_all(jnp.stack([fields] * lax.axis_size('section')), 'section',...  9.11 us
    all_to_all x1, waiting for transfers between devices, local(): lax.all_to_all(normed_half, 'tile', split_axis=0, concat_axis=1, tiled=True)  6.38 us
    ppermute x2, starting transfers between devices, from_behind(): return lax.ppermute(block, axis, route)  5.25 us
  transfers between devices with their start and end apart: 6, of which 6 were waited for; matrix products, arithmetic and copies ran while one was open for 13% of the time, Pallas kernels for 0%

profile of v1, /device:TPU:1, one launch (start us, length us, event | category | flops | bytes accessed | tf_op | source)
XLA Modules:
  0.0 182.7 jit_solution(571520774312521849)
XLA Ops:
  8.3 2.5 %convolution_convert_fusion = bf16[1536,192]{0,1:T(8,128)(2,1)} fusion(bf16[384,192]{1,0:T(8,128)(2,1)} %bitcast.144, s32[1536]{0:T(1024)S(1)} %fusion.98), kind=kOutput, calls=%fused_computation.14 | convolution fusion | flops 227377152 | bytes 743424 | tf_op jit(solution)/shard_map/dot_general | solution.py:28
  10.8 3.5 %fusion.8 = bf16[768,1536,1]{1,0,2:T(8,128)(2,1)} fusion(s32[1536]{0:T(1024)S(1)} %get-tuple-element.41, s32[768]{0:T(1024)S(1)} %get-tuple-element.42, bf16[48,96]{1,0:T(8,128)(2,1)} %bitcast.145, s32[1536]{0:T(1024)S(1)} %get-tuple-element.40, s32[768]{0:T(1024)S(1)} %get-tuple-element.43), kind=kOutput, calls=%fused_computation.11 | convolution fusion | flops 237367296 | bytes 2386944 | tf_op jit(solution)/shard_map/dot_general | solution.py:35
  14.3 5.1 %fusion.7 = bf16[3,192,1536]{2,1,0:T(8,128)(2,1)} fusion(bf16[768,1536,1]{1,0,2:T(8,128)(2,1)} %fusion.8, f32[1536]{0:T(1024)S(1)} %add.318, bf16[3,384,768]{2,1,0:T(8,128)(2,1)S(1)} %copy-done, s32[]{:T(128)S(6)} %select_n.229), kind=kOutput, calls=%fused_computation.10 | convolution fusion | flops 1367801856 | bytes 5021700 | tf_op jit(solution)/shard_map/zji,if->zjf/dot_general | solution.py:85
  19.3 4.3 %fusion.17 = bf16[3,192,768]{2,1,0:T(8,128)(2,1)S(1)} fusion(bf16[3,192,1536]{2,1,0:T(8,128)(2,1)} %fusion.7, bf16[1536,192]{0,1:T(8,128)(2,1)} %convolution_convert_fusion, s32[768]{0:T(1024)S(1)} %get-tuple-element.45, s32[1536]{0:T(1024)S(1)} %fusion.91, f32[768]{0:T(1024)S(1)} %add.331, s32[768]{0:T(1024)S(1)} %get-tuple-element.44), kind=kOutput, calls=%fused_computation.23 | convolution fusion | flops 1820049408 | bytes 3259392 | tf_op jit(solution)/shard_map/zji,if->zjf/dot_general | solution.py:94
  28.9 4.0 %collective-permute-start.1 = (bf16[1,193,768]{2,1,0:T(8,128)(2,1)S(1)}, bf16[1,193,768]{2,1,0:T(8,128)(2,1)S(1)}, u32[]{:S(2)}, u32[]{:S(2)}) collective-permute-start(bf16[1,193,768]{2,1,0:T(8,128)(2,1)S(1)} %pad_maximum_fusion.9), channel_id=1, source_target_pairs={{0,1},{1,2},{2,3},{3,4},{4,5},{5,6},{6,7},{7,8},{8,9},{9,10},{10,1... | collective-permute-start | bytes 889352 | tf_op jit(solution)/shard_map/ppermute | solution.py:13
  36.4 1.9 %collective-permute-done.1 = bf16[1,193,768]{2,1,0:T(8,128)(2,1)S(1)} collective-permute-done((bf16[1,193,768]{2,1,0:T(8,128)(2,1)S(1)}, bf16[1,193,768]{2,1,0:T(8,128)(2,1)S(1)}, u32[]{:S(2)}, u32[]{:S(2)}) %collective-permute-start.1) | collective-permute-done | bytes 296480 | tf_op jit(solution)/shard_map/ppermute | solution.py:13
  43.1 17.3 %all-to-all-start = ((bf16[384,3,192]{2,1,0:T(4,128)(2,1)}), bf16[384,3,192]{2,1,0:T(4,128)(2,1)S(1)}, u32[]{:S(2)}, u32[]{:S(2)}) async-start(bf16[384,3,192]{2,1,0:T(4,128)(2,1)} %copy.34), calls=%async_computation | async-start | bytes 1572864 | tf_op jit(solution)/shard_map/all_to_all | solution.py:183
  60.4 2.8 %constant_dynamic-slice_fusion = (bf16[3,1,384,192]{3,2,1,0:T(8,128)(2,1)}, bf16[3,1,384,192]{3,2,1,0:T(8,128)(2,1)}) fusion(bf16[3,2,384,384]{3,2,1,0:T(8,128)(2,1)} %param.17, s32[]{:T(128)S(6)} %select_n.229, s32[]{:T(128)S(6)} %add.349), kind=kLoop, calls=%fused_computation.233 | loop fusion | bytes 1769480 | tf_op jit(solution)/shard_map/slice | solution.py:141
  63.2 2.1 %copy.57 = bf16[3,1,384,192]{2,3,1,0:T(8,128)(2,1)} copy(bf16[3,1,384,192]{3,2,1,0:T(8,128)(2,1)} %get-tuple-element.7) | data formatting | bytes 884736
  65.3 2.1 %copy.58 = bf16[3,1,384,192]{2,3,1,0:T(8,128)(2,1)} copy(bf16[3,1,384,192]{3,2,1,0:T(8,128)(2,1)} %get-tuple-element.8) | data formatting | bytes 884736
  71.0 2.3 %fusion.74 = bf16[384,1,384]{2,0,1:T(8,128)(2,1)S(1)} fusion(), kind=kLoop, calls=%fused_computation.132 | loop fusion | flops 1916928 | bytes 294912 | tf_op jit(solution)/shard_map/neg | solution.py:197
  73.4 2.6 %sine_convert_fusion = (bf16[384,1,384]{2,0,1:T(8,128)(2,1)S(1)}, bf16[384,1,384]{2,0,1:T(8,128)(2,1)S(1)}) fusion(), kind=kLoop, calls=%fused_computation.93 | loop fusion | flops 1622016 | bytes 589824 | tf_op jit(solution)/shard_map/convert_element_type | solution.py:20
  77.4 6.4 %all-to-all-done = bf16[384,3,192]{2,1,0:T(4,128)(2,1)S(1)} async-done(((bf16[384,3,192]{2,1,0:T(4,128)(2,1)}), bf16[384,3,192]{2,1,0:T(4,128)(2,1)S(1)}, u32[]{:S(2)}, u32[]{:S(2)}) %all-to-all-start) | async-done | bytes 442400 | tf_op jit(solution)/shard_map/all_to_all | solution.py:183
  85.0 2.2 %stack.133 = bf16[1,3,384,192]{3,2,1,0:T(8,128)(2,1)} reshape(bf16[3,128,3,192]{3,2,1,0:T(4,128)(2,1)} %copy.36) | data formatting | bytes 884736 | tf_op jit(solution)/shard_map/stack | solution.py:185
  90.0 9.1 %all_to_all.29 = bf16[2,3,384,192]{2,3,1,0:T(8,128)(2,1)S(1)} all-to-all(bf16[2,3,384,192]{2,3,1,0:T(8,128)(2,1)} %copy.37), channel_id=1, replica_groups=mesh['section'=2,'tile'=128] {'section'}, dimensions={0} | all-to-all | bytes 1769472 | tf_op jit(solution)/shard_map/all_to_all | solution.py:185
  100.2 4.0 %fusion.21 = bf16[3,2,384,192]{2,3,1,0:T(8,128)(2,1)} fusion(bf16[1,384,2,384]{3,1,2,0:T(8,128)(2,1)} %get-tuple-element.29, bf16[1,384,2,384]{3,1,2,0:T(8,128)(2,1)} %get-tuple-element.22, bf16[3,384,384,1]{1,2,3,0:T(8,128)(2,1)} %bitcast.143, bf16[384,1,192]{0,2,1:T(8,128)(2,1)S(1)} %copy-done.10, bf16[384,1,192]{0,2,1:T(8,128)(2,1)S(1)} %copy-done.9), kind=kOutput, calls=%fused_computation.35 | convolution fusion | flops 1023049728 | bytes 3244032 | tf_op jit(solution)/shard_map/puqh,chqw->cpuw/dot_general | solution.py:136
  105.8 1.8 fusion.22
  107.6 9.3 %all-gather.2.cloned.1.call-done = bf16[3,384,2,384]{1,3,2,0:T(8,128)(2,1)} async-done(((bf16[3,384,2,192]{1,3,2,0:T(8,128)(2,1)}), bf16[3,384,2,384]{1,3,2,0:T(8,128)(2,1)}) %all-gather.2.cloned.1.call-update) | async-done | bytes 1769488 | tf_op jit(solution)/shard_map/all_gather | solution.py:208
  117.0 2.0 %fusion.24 = bf16[3,384,192]{1,2,0:T(8,128)(2,1)S(1)} fusion(bf16[3,384,2,384]{1,3,2,0:T(8,128)(2,1)} %all-gather.2.cloned.1.call-done, bf16[1,384,192]{1,2,0:T(8,128)(2,1)S(1)} %copy-done.8, bf16[1,384,192]{1,2,0:T(8,128)(2,1)S(1)} %get-tuple-element.18), kind=kOutput, calls=%fused_computation.39 | convolution fusion | flops 340770816 | bytes 2506752 | tf_op jit(solution)/shard_map/chqw,qwv->chv/dot_general | solution.py:209
  120.4 13.6 %all-to-all-start.2 = ((bf16[3,384,192]{2,0,1:T(4,128)(2,1)}), bf16[3,384,192]{2,0,1:T(4,128)(2,1)S(1)}, u32[]{:S(2)}, u32[]{:S(2)}) async-start(bf16[3,384,192]{2,0,1:T(4,128)(2,1)} %copy.40), calls=%async_computation.2 | async-start | bytes 1572864 | tf_op jit(solution)/shard_map/all_to_all | solution.py:213
  134.0 25.4 %all-to-all-done.2 = bf16[3,384,192]{2,0,1:T(4,128)(2,1)S(1)} async-done(((bf16[3,384,192]{2,0,1:T(4,128)(2,1)}), bf16[3,384,192]{2,0,1:T(4,128)(2,1)S(1)}, u32[]{:S(2)}, u32[]{:S(2)}) %all-to-all-start.2) | async-done | bytes 442400 | tf_op jit(solution)/shard_map/all_to_all | solution.py:213
  163.5 3.4 %copy.43 = f32[128,3,3,192]{3,1,0,2:T(4,128)} copy(f32[128,3,3,192]{3,2,0,1:T(4,128)} %bitcast.137) | data formatting | bytes 1769472 | tf_op jit(solution)/shard_map/convert_element_type | solution.py:214
  166.9 1.8 reshape.342
  171.5 1.9 %collective-permute-start.2 = (bf16[192,3,192]{0,2,1:T(8,128)(2,1)S(1)}, bf16[192,3,192]{0,2,1:T(8,128)(2,1)S(1)}, u32[]{:S(2)}, u32[]{:S(2)}) collective-permute-start(bf16[192,3,192]{0,2,1:T(8,128)(2,1)S(1)} %get-tuple-element.27), channel_id=1, source_target_pairs={{0,128},{128,0},{1,129},{129,1},{2,130},{130,2},{3,131},{131,3},{4... | collective-permute-start | bytes 663560 | tf_op jit(solution)/shard_map/ppermute | solution.py:217
  (78 shorter events, 37.8 us)
Async XLA Ops:
  6.5 7.7 %copy-start = (bf16[3,384,768]{2,1,0:T(8,128)(2,1)S(1)}, bf16[3,384,768]{2,1,0:T(8,128)(2,1)}, u32[]{:S(2)}) copy-start(bf16[3,384,768]{2,1,0:T(8,128)(2,1)} %param.9) | copy-start | bytes 5308420
  23.6 5.2 %collective-permute-start = (bf16[3,1,768]{2,1,0:T(2,128)(2,1)S(1)}, bf16[3,1,768]{2,1,0:T(2,128)(2,1)S(1)}, u32[]{:S(2)}, u32[]{:S(2)}) collective-permute-start(bf16[3,1,768]{2,1,0:T(2,128)(2,1)S(1)} %slice.72), channel_id=1, source_target_pairs={{0,128},{1,129},{2,130},{3,131},{4,132},{5,133},{6,134},{7,135},{8... | collective-permute-start | bytes 13832 | tf_op jit(solution)/shard_map/ppermute | solution.py:13
  28.9 9.4 %collective-permute-start.1 = (bf16[1,193,768]{2,1,0:T(8,128)(2,1)S(1)}, bf16[1,193,768]{2,1,0:T(8,128)(2,1)S(1)}, u32[]{:S(2)}, u32[]{:S(2)}) collective-permute-start(bf16[1,193,768]{2,1,0:T(8,128)(2,1)S(1)} %pad_maximum_fusion.9), channel_id=1, source_target_pairs={{0,1},{1,2},{2,3},{3,4},{4,5},{5,6},{6,7},{7,8},{8,9},{9,10},{10,1... | collective-permute-start | bytes 889352 | tf_op jit(solution)/shard_map/ppermute | solution.py:13
  36.4 2.1 %copy-start.3 = (bf16[2,2,192,384]{3,2,1,0:T(8,128)(2,1)S(1)}, bf16[2,2,192,384]{3,2,1,0:T(8,128)(2,1)}, u32[]{:S(2)}) copy-start(bf16[2,2,192,384]{3,2,1,0:T(8,128)(2,1)} %stack.132) | copy-start | bytes 1769476
  38.5 1.1 copy-start.1
  39.1 1.1 copy-start.2
  39.2 1.1 copy-start.11
  40.3 1.2 copy-start.12
  43.1 40.7 %all-to-all-start = ((bf16[384,3,192]{2,1,0:T(4,128)(2,1)}), bf16[384,3,192]{2,1,0:T(4,128)(2,1)S(1)}, u32[]{:S(2)}, u32[]{:S(2)}) async-start(bf16[384,3,192]{2,1,0:T(4,128)(2,1)} %copy.34), calls=%async_computation | async-start | bytes 1572864 | tf_op jit(solution)/shard_map/all_to_all | solution.py:183
  60.4 56.6 %all-gather.2.cloned.1.call-start = ((), (), s32[]{:S(2)}) async-start(), calls=%async_computation.3 | async-start | bytes 2654208 | tf_op jit(solution)/shard_map/all_gather | solution.py:208
  90.0 10.1 %copy-start.9 = (bf16[384,1,192]{0,2,1:T(8,128)(2,1)S(1)}, bf16[384,1,192]{0,2,1:T(8,128)(2,1)}, u32[]{:S(2)}) copy-start(bf16[384,1,192]{0,2,1:T(8,128)(2,1)} %get-tuple-element.19) | copy-start | bytes 442372
  90.0 10.1 %copy-start.10 = (bf16[384,1,192]{0,2,1:T(8,128)(2,1)S(1)}, bf16[384,1,192]{0,2,1:T(8,128)(2,1)}, u32[]{:S(2)}) copy-start(bf16[384,1,192]{0,2,1:T(8,128)(2,1)} %get-tuple-element.21) | copy-start | bytes 442372
  100.2 4.0 %copy-start.4 = (bf16[3,1,384,192]{2,3,1,0:T(8,128)(2,1)S(1)}, bf16[3,1,384,192]{2,3,1,0:T(8,128)(2,1)}, u32[]{:S(2)}) copy-start(bf16[3,1,384,192]{2,3,1,0:T(8,128)(2,1)} %copy.57) | copy-start | bytes 1327108
  100.2 4.0 %copy-start.5 = (bf16[3,1,384,192]{2,3,1,0:T(8,128)(2,1)S(1)}, bf16[3,1,384,192]{2,3,1,0:T(8,128)(2,1)}, u32[]{:S(2)}) copy-start(bf16[3,1,384,192]{2,3,1,0:T(8,128)(2,1)} %copy.58) | copy-start | bytes 1327108
  104.2 1.6 copy-start.6
  104.2 1.6 copy-start.7
  105.8 11.2 %copy-start.8 = (bf16[1,384,192]{1,2,0:T(8,128)(2,1)S(1)}, bf16[1,384,192]{1,2,0:T(8,128)(2,1)}, u32[]{:S(2)}) copy-start(bf16[1,384,192]{1,2,0:T(8,128)(2,1)} %get-tuple-element.20) | copy-start | bytes 442372
  120.4 39.0 %all-to-all-start.2 = ((bf16[3,384,192]{2,0,1:T(4,128)(2,1)}), bf16[3,384,192]{2,0,1:T(4,128)(2,1)S(1)}, u32[]{:S(2)}, u32[]{:S(2)}) async-start(bf16[3,384,192]{2,0,1:T(4,128)(2,1)} %copy.40), calls=%async_computation.2 | async-start | bytes 1572864 | tf_op jit(solution)/shard_map/all_to_all | solution.py:213
  171.5 3.2 %collective-permute-start.2 = (bf16[192,3,192]{0,2,1:T(8,128)(2,1)S(1)}, bf16[192,3,192]{0,2,1:T(8,128)(2,1)S(1)}, u32[]{:S(2)}, u32[]{:S(2)}) collective-permute-start(bf16[192,3,192]{0,2,1:T(8,128)(2,1)S(1)} %get-tuple-element.27), channel_id=1, source_target_pairs={{0,128},{128,0},{1,129},{129,1},{2,130},{130,2},{3,131},{131,3},{4... | collective-permute-start | bytes 663560 | tf_op jit(solution)/shard_map/ppermute | solution.py:217
Sparse Core Ops, SparseCore 0:
  107.8 9.1 all-gather.1
